TPU v7x, 32 devices: a whole 2x2x4 slice. The times are simulated.
32 devices in a mesh: wide: 8 (over z, y), mp: 4 (over x, core).
Axes of the slice: x: 2, y: 2, z: 4, core: 2. Of those that a mesh axis runs over, the one named last changes fastest.
Arguments:
- clip_feats: bfloat16 [1024, 768], P('wide'), may hold values from -6 to 6
- teacher_audio: bfloat16 [1024, 512], P('wide'), may hold values from -16 to 16
- teacher_text: bfloat16 [1024, 512], P(('wide', 'mp')), may hold values from -16 to 16
- w_first: bfloat16 [768, 512], P(None, 'mp'), may hold values from -0.21875 to 0.21875
- w_second: bfloat16 [512, 512], P('mp'), may hold values from -0.25 to 0.25
- pairing: int32 [1024], P('wide'), may hold values from 0 to 1023
Outputs:
- loss: float32 [], replicated
- grad_first: float32 [768, 512], P(None, 'mp')
- grad_second: float32 [512, 512], P('mp')
All inputs are finite; a program needn't handle non-finite values.
Results may differ from a plain program's by a relative error of at most 0.0052.
Values may be sent and summed in bfloat16 or wider, within the bound.
No kernel may reach another device: no remote copies, remote signals or barrier semaphores. Data moves between devices by JAX's collectives and lax.ppermute only.
A program may use at most 64 MiB of HBM per device.

v0:
```python
import math
import jax
import jax.numpy as jnp
from jax import lax
from jax.sharding import PartitionSpec as P

teacher_scale = 14.0
student_scale = 64.0
eps = 1e-06


def normalize(values):
    return values / jnp.sqrt(jnp.sum(values * values, axis=1, keepdims=True) + eps)


def inner_rows(left, right):
    return lax.dot_general(
        left, right, (((1,), (1,)), ((), ())), preferred_element_type=jnp.float32
    )


def sweep(work, initial, source, base):
    count = source.shape[0]
    width = math.gcd(count, 2048)
    block_count = count // width

    def advance(index, carry):
        block = lax.dynamic_slice_in_dim(source, index * width, width, 0)
        return work(carry, block, base + index * width)

    return lax.fori_loop(0, block_count, advance, initial)


def body(clip_feats, teacher_audio, teacher_text, w_first, w_second, pairing):
    row_count = clip_feats.shape[0]
    total = row_count * lax.axis_size("wide")
    quarter = teacher_text.shape[0]
    mp_size = lax.axis_size("mp")
    mp_index = lax.axis_index("mp")
    pre_act = jnp.dot(clip_feats, w_first, preferred_element_type=jnp.float32)
    gelu_out, gelu_back = jax.vjp(lambda u: jax.nn.gelu(u, approximate=False), pre_act)
    hidden = gelu_out.astype(jnp.bfloat16)
    raw = lax.psum(jnp.dot(hidden, w_second, preferred_element_type=jnp.float32), "mp")
    norm = jnp.sqrt(jnp.sum(raw * raw, axis=1, keepdims=True) + eps)
    student = raw / norm
    stacked = jnp.concatenate(
        [
            normalize(teacher_audio.astype(jnp.float32)).astype(jnp.bfloat16),
            student.astype(jnp.bfloat16),
        ],
        axis=0,
    )
    capt_local = normalize(teacher_text.astype(jnp.float32)).astype(jnp.bfloat16)

    def logits(block, start):
        scores = inner_rows(stacked, block)
        local_ids = start + jnp.arange(block.shape[0], dtype=jnp.int32)
        global_ids = (
            local_ids // quarter * (quarter * mp_size) + mp_index * quarter + local_ids % quarter
        )
        hit = global_ids[None, :] == pairing[:, None]
        return (teacher_scale * scores[:row_count], student_scale * scores[row_count:], hit)

    def first_pass(carry, block, start):
        tlog, slog, hit = logits(block, start)
        texp = jnp.exp(tlog)
        sexp = jnp.exp(slog)
        return (
            carry[0] + jnp.sum(texp, axis=1),
            carry[1] + jnp.sum(sexp, axis=1),
            carry[2] + jnp.sum(texp * (tlog - slog), axis=1),
            carry[3] + jnp.sum(jnp.where(hit, slog, 0.0), axis=1),
        )

    zeros_row = jnp.zeros((row_count,), jnp.float32)
    first_init = (zeros_row, zeros_row, zeros_row, zeros_row)
    zeros_grad = jnp.zeros((row_count, stacked.shape[1]), jnp.float32)

    def make_second(zt_sum, zs_sum):

        def second_pass(carry, block, start):
            tlog, slog, hit = logits(block, start)
            coef = (
                2.0 * jnp.exp(slog) / zs_sum[:, None]
                - jnp.exp(tlog) / zt_sum[:, None]
                - hit.astype(jnp.float32)
            ).astype(jnp.bfloat16)
            return carry + jnp.dot(coef, block, preferred_element_type=jnp.float32)

        return second_pass

    gathered = lax.all_gather(capt_local, "wide", axis=0, tiled=True)
    partial_stats = sweep(first_pass, first_init, gathered, 0)
    zt_sum, zs_sum, acc_sum, spair = lax.psum(partial_stats, "mp")
    second_pass = make_second(zt_sum, zs_sum)
    dpart = sweep(second_pass, zeros_grad, gathered, 0)
    loss_part = jnp.sum(acc_sum / zt_sum - jnp.log(zt_sum) + 2.0 * jnp.log(zs_sum) - spair)
    dstud = lax.psum(dpart, "mp") * (student_scale / total)
    draw = ((dstud - student * jnp.sum(student * dstud, axis=1, keepdims=True)) / norm).astype(
        jnp.bfloat16
    )
    grad_second = jnp.dot(hidden.T, draw, preferred_element_type=jnp.float32)
    dhid = lax.dot_general(
        draw, w_second, (((1,), (1,)), ((), ())), preferred_element_type=jnp.float32
    )
    dpre = gelu_back(dhid)[0].astype(jnp.bfloat16)
    grad_first = jnp.dot(clip_feats.T, dpre, preferred_element_type=jnp.float32)
    grad_first, grad_second, loss_sum = lax.psum((grad_first, grad_second, loss_part), "wide")
    return (loss_sum / total, grad_first, grad_second)


def solution(mesh):
    return jax.shard_map(
        body,
        mesh=mesh,
        in_specs=(
            P("wide", None),
            P("wide", None),
            P(("wide", "mp"), None),
            P(None, "mp"),
            P("mp", None),
            P("wide"),
        ),
        out_specs=(P(), P(None, "mp"), P("mp", None)),
        check_vma=False,
    )
```

profile of v0, /device:TPU:0, one launch (start us, length us, event | category | flops | bytes accessed | tf_op | source)
XLA Modules:
  0.0 175.5 jit_solution(1740384706962114284)
XLA Ops:
  7.2 0.0 copy-start
  7.2 0.0 copy-start.5
  7.2 0.0 all-reduce.6.cloned.1.call-start
  7.2 0.9 copy-done
  8.1 1.3 multiply_convert_fusion
  9.4 0.0 copy-done.5
  9.4 0.9 fusion.47
  10.2 0.0 copy-start.3
  10.2 0.0 all-reduce.6.cloned.1.call-update
  10.3 0.0 all-reduce.8.cloned.1.call-start
  10.3 0.8 copy-done.3
  11.1 0.0 copy-start.6
  11.1 0.1 fusion
  11.3 0.6 copy-done.6
  11.9 0.1 fusion.13
  12.0 0.1 fusion.14
  12.1 0.1 fusion.1
  12.2 32.6 %all_gather.3 = bf16[256,512]{1,0:T(8,128)(2,1)S(1)} all-gather(bf16[32,512]{1,0:T(8,128)(2,1)S(1)} %fusion.14), channel_id=1, replica_groups=mesh['wide'=8,'mp'=4] {'wide'}, dimensions={0}, use_global_device_ids=true | all-gather | bytes 294912 | tf_op jit(solution)/shard_map/all_gather | solution.py:92
  44.8 1.1 all-reduce.6.cloned.1.call-done
  45.9 0.0 copy-start.1
  45.9 1.1 multiply_reduce_fusion.1
  47.1 0.0 copy-done.1
  47.1 0.1 fusion.43
  47.2 0.0 copy-start.7
  47.2 0.3 fusion.2
  47.5 0.4 copy-done.7
  47.8 0.1 multiply_reduce_fusion.2
  48.0 5.8 %all-reduce.1 = (f32[128]{0:T(128)S(1)}, f32[128]{0:T(128)S(1)}, f32[128]{0:T(128)S(1)}, f32[128]{0:T(128)S(1)}) all-reduce(f32[128]{0:T(128)S(1)} %get-tuple-element.46, f32[128]{0:T(128)S(1)} %get-tuple-element.47, f32[128]{0:T(128)S(1)} %get-tuple-element.48, f32[128]{0:T(128)S(1)} %get-tuple-element.45), channel_id=1, replica_groups=mesh['wide'=8,'mp'=4] {'mp'}, use_global_device_ids=true, to_apply=%region_11.12 | all-reduce | flops 512 | bytes 4096 | tf_op jit(solution)/shard_map/psum | solution.py:94
  53.7 1.0 fusion.11
  54.7 0.0 all-reduce.8.cloned.1.call-update
  54.7 0.0 all-reduce.10.cloned.1.call-start
  54.8 32.4 %all-reduce.8.cloned.1.call-done = f32[128,512]{1,0:T(8,128)} async-done(((f32[128,512]{1,0:T(8,128)}), f32[128,512]{1,0:T(8,128)}) %all-reduce.8.cloned.1.call-update) | async-done | bytes 262160 | tf_op jit(solution)/shard_map/psum | solution.py:98
  87.2 0.0 copy-start.2
  87.2 1.2 multiply_reduce_fusion
  88.4 0.0 copy-done.2
  88.4 0.1 divide_convert_fusion
  88.6 0.9 fusion.48
  89.5 1.3 convolution_bitcast_fusion
  90.7 0.0 all-reduce.10.cloned.1.call-update
  90.8 0.6 subtract_reduce_fusion
  91.4 22.2 %psum.68 = f32[]{:T(128)} all-reduce(f32[]{:T(128)} %subtract_reduce_fusion), channel_id=1, replica_groups=mesh['wide'=8,'mp'=4] {'wide'}, use_global_device_ids=true, to_apply=%region_13.14 | all-reduce | flops 1 | bytes 8 | tf_op jit(solution)/shard_map/psum | solution.py:108
  114.3 50.9 %all-reduce.10.cloned.1.call-done = (f32[768,128]{0,1:T(8,128)}, f32[128,512]{1,0:T(8,128)}) async-done(((f32[768,128]{0,1:T(8,128)}, f32[128,512]{1,0:T(8,128)}), (f32[768,128]{0,1:T(8,128)}, f32[128,512]{1,0:T(8,128)})) %all-reduce.10.cloned.1.call-update) | async-done | bytes 655376 | tf_op jit(solution)/shard_map/psum | solution.py:108
  165.2 0.0 copy-start.4
  165.2 2.0 %copy.9 = f32[768,128]{1,0:T(8,128)} copy(f32[768,128]{0,1:T(8,128)} %get-tuple-element.58) | data formatting | bytes 786432
  167.1 0.0 copy-done.4
  167.1 0.7 copy.14
  (4 shorter events, 0.0 us)
Async XLA Ops:
  7.2 0.9 copy-start
  7.2 2.2 %copy-start.5 = (bf16[128,512]{1,0:T(8,128)(2,1)S(1)}, bf16[128,512]{1,0:T(8,128)(2,1)}, u32[]{:S(2)}) copy-start(bf16[128,512]{1,0:T(8,128)(2,1)} %param.10) | copy-start | bytes 393220
  7.2 38.7 %all-reduce.6.cloned.1.call-start = ((), (), s32[]{:S(2)}) async-start(), calls=%async_computation | async-start | bytes 524288 | tf_op jit(solution)/shard_map/psum | solution.py:43
  10.2 0.9 copy-start.3
  10.3 76.9 %all-reduce.8.cloned.1.call-start = ((), (), s32[]{:S(2)}) async-start(), calls=%async_computation.1 | async-start | bytes 524288 | tf_op jit(solution)/shard_map/psum | solution.py:98
  11.1 0.8 copy-start.6
  45.9 1.1 copy-start.1
  47.2 0.7 copy-start.7
  54.7 110.4 %all-reduce.10.cloned.1.call-start = ((), (), s32[]{:S(2)}) async-start(), calls=%async_computation.2 | async-start | bytes 1310720 | tf_op jit(solution)/shard_map/psum | solution.py:108
  87.2 1.2 copy-start.2
  165.2 2.0 %copy-start.4 = (f32[128,512]{1,0:T(8,128)S(1)}, f32[128,512]{1,0:T(8,128)}, u32[]{:S(2)}) copy-start(f32[128,512]{1,0:T(8,128)} %get-tuple-element.77) | copy-start | bytes 786436
Sparse Core Ops, SparseCore 0:
  10.9 34.9 all-reduce.5
  54.9 32.3 all-reduce.7
  91.3 73.8 all-reduce.9
where the time goes:
time: 176 us; the launch traced here: 175 us
  waiting for transfers between devices  84.5 us (48%)
  blocking collectives  60.5 us (34%)
  between operations  15.7 us (9%)
  matrix products  5.56 us (3%)
  local copies, waits for them, and re-layouts  5.38 us (3%)
  other arithmetic  3.71 us (2%)
    psum x1, waiting for transfers between devices, body(): lax.psum((grad_first, grad_second, loss_part), 'wide')  50.9 us
    all_gather x1, blocking collectives, body(): gathered = lax.all_gather(capt_local, 'wide', axis=0, tiled=True)  32.6 us
    psum x1, waiting for transfers between devices, body(): dstud = lax.psum(dpart, 'mp') * (student_scale / total)  32.4 us
    psum x1, blocking collectives, body(): lax.psum((grad_first, grad_second, loss_part), 'wide')  22.2 us
    psum x1, blocking collectives, body(): zt_sum, zs_sum, acc_sum, spair = lax.psum(partial_stats, 'mp')  5.76 us
    unnamed x18, local copies, waits for them, and re-layouts  5.38 us
  transfers between devices with their start and end apart: 3, of which 3 were waited for; matrix products, arithmetic and copies ran while one was open for 1% of the time, Pallas kernels for 0%

commit v1 on v0

--- a/solution.py
+++ b/solution.py
@@ -95,7 +95,11 @@
     second_pass = make_second(zt_sum, zs_sum)
     dpart = sweep(second_pass, zeros_grad, gathered, 0)
     loss_part = jnp.sum(acc_sum / zt_sum - jnp.log(zt_sum) + 2.0 * jnp.log(zs_sum) - spair)
-    dstud = lax.psum(dpart, "mp") * (student_scale / total)
+
+    def _solve_heads(frame):
+        return lax.all_gather(frame, axis_name="mp").sum(axis=0)
+
+    dstud = _solve_heads(dpart) * (student_scale / total)
     draw = ((dstud - student * jnp.sum(student * dstud, axis=1, keepdims=True)) / norm).astype(
         jnp.bfloat16
     )

time: 176 us -> 160 us (0.909)
  waiting for transfers between devices: 84.5 us -> 68.6 us
    psum x1 -> x0, waiting for transfers between devices: 32.4 us -> none  [body(): dstud = lax.psum(dpart, 'mp') * (student_scale / total)]
    all_gather x0 -> x1, waiting for transfers between devices: none -> 16.8 us  [_solve_heads(): return lax.all_gather(frame, axis_name='mp').sum(axis=0)]
    unnamed x18 -> x16, local copies, waits for them, and re-layouts: 5.38 us -> 5.38 us
where the time goes in v1:
time: 160 us
  waiting for transfers between devices  68.6 us (43%)
  blocking collectives  60.5 us (38%)
  between operations  15.7 us (10%)
  matrix products  5.56 us (3%)
  local copies, waits for them, and re-layouts  5.38 us (3%)
  other arithmetic  4.02 us (3%)
    psum x1, waiting for transfers between devices, body(): lax.psum((grad_first, grad_second, loss_part), 'wide')  50.5 us
    all_gather x1, blocking collectives, body(): gathered = lax.all_gather(capt_local, 'wide', axis=0, tiled=True)  32.6 us
    psum x1, blocking collectives, body(): lax.psum((grad_first, grad_second, loss_part), 'wide')  22.2 us
    all_gather x1, waiting for transfers between devices, _solve_heads(): return lax.all_gather(frame, axis_name='mp').sum(axis=0)  16.8 us
    psum x1, blocking collectives, body(): zt_sum, zs_sum, acc_sum, spair = lax.psum(partial_stats, 'mp')  5.76 us
    unnamed x16, local copies, waits for them, and re-layouts  5.38 us
  transfers between devices with their start and end apart: 3, of which 3 were waited for; matrix products, arithmetic and copies ran while one was open for 1% of the time, Pallas kernels for 0%

profile of v1, /device:TPU:0, one launch (start us, length us, event | category | flops | bytes accessed | tf_op | source)
XLA Modules:
  0.0 159.8 jit_solution(12057231874256509596)
XLA Ops:
  7.2 0.0 copy-start
  7.2 0.0 copy-start.4
  7.2 0.0 all-reduce.5.cloned.1.call-start
  7.2 0.9 copy-done
  8.1 1.3 multiply_convert_fusion
  9.4 0.0 copy-done.4
  9.4 0.9 fusion.47
  10.2 0.0 copy-start.2
  10.2 0.0 all-reduce.5.cloned.1.call-update
  10.3 0.0 all-gather.3.cloned.1.call-start
  10.3 0.8 copy-done.2
  11.1 0.0 copy-start.5
  11.1 0.1 fusion
  11.3 0.6 copy-done.5
  11.9 0.1 fusion.13
  12.0 0.1 fusion.14
  12.1 0.1 fusion.1
  12.2 32.6 %all_gather.9 = bf16[256,512]{1,0:T(8,128)(2,1)S(1)} all-gather(bf16[32,512]{1,0:T(8,128)(2,1)S(1)} %fusion.14), channel_id=1, replica_groups=mesh['wide'=8,'mp'=4] {'wide'}, dimensions={0}, use_global_device_ids=true | all-gather | bytes 294912 | tf_op jit(solution)/shard_map/all_gather | solution.py:92
  44.8 1.1 all-reduce.5.cloned.1.call-done
  45.9 0.0 copy-start.1
  45.9 1.1 multiply_reduce_fusion.1
  47.1 0.0 copy-done.1
  47.1 0.1 fusion.43
  47.2 0.0 copy-start.6
  47.2 0.3 fusion.2
  47.5 0.4 copy-done.6
  47.8 0.1 multiply_reduce_fusion.2
  48.0 5.8 %all-reduce.1 = (f32[128]{0:T(128)S(1)}, f32[128]{0:T(128)S(1)}, f32[128]{0:T(128)S(1)}, f32[128]{0:T(128)S(1)}) all-reduce(f32[128]{0:T(128)S(1)} %get-tuple-element.46, f32[128]{0:T(128)S(1)} %get-tuple-element.47, f32[128]{0:T(128)S(1)} %get-tuple-element.48, f32[128]{0:T(128)S(1)} %get-tuple-element.45), channel_id=1, replica_groups=mesh['wide'=8,'mp'=4] {'mp'}, use_global_device_ids=true, to_apply=%region_11.12 | all-reduce | flops 512 | bytes 4096 | tf_op jit(solution)/shard_map/psum | solution.py:94
  53.7 1.0 fusion.11
  54.7 0.0 all-gather.3.cloned.1.call-update
  54.7 0.0 all-reduce.7.cloned.1.call-start
  54.8 16.8 %all-gather.3.cloned.1.call-done = f32[512,512]{1,0:T(8,128)} async-done(((f32[128,512]{1,0:T(8,128)}), f32[512,512]{1,0:T(8,128)}) %all-gather.3.cloned.1.call-update) | async-done | bytes 1048592 | tf_op jit(solution)/shard_map/all_gather | solution.py:100
  71.6 1.3 reduce_sum.102
  73.0 0.2 multiply_reduce_fusion
  73.2 0.1 divide_convert_fusion
  73.3 0.9 fusion.48
  74.2 1.3 convolution_bitcast_fusion
  75.5 0.0 all-reduce.7.cloned.1.call-update
  75.5 0.6 subtract_reduce_fusion
  76.1 22.2 %psum.61 = f32[]{:T(128)} all-reduce(f32[]{:T(128)} %subtract_reduce_fusion), channel_id=1, replica_groups=mesh['wide'=8,'mp'=4] {'wide'}, use_global_device_ids=true, to_apply=%region_13.14 | all-reduce | flops 1 | bytes 8 | tf_op jit(solution)/shard_map/psum | solution.py:112
  99.0 50.5 %all-reduce.7.cloned.1.call-done = (f32[768,128]{0,1:T(8,128)}, f32[128,512]{1,0:T(8,128)}) async-done(((f32[768,128]{0,1:T(8,128)}, f32[128,512]{1,0:T(8,128)}), (f32[768,128]{0,1:T(8,128)}, f32[128,512]{1,0:T(8,128)})) %all-reduce.7.cloned.1.call-update) | async-done | bytes 655376 | tf_op jit(solution)/shard_map/psum | solution.py:112
  149.5 0.0 copy-start.3
  149.5 2.0 %copy.9 = f32[768,128]{1,0:T(8,128)} copy(f32[768,128]{0,1:T(8,128)} %get-tuple-element.58) | data formatting | bytes 786432
  151.5 0.0 copy-done.3
  151.5 0.7 copy.13
  (4 shorter events, 0.0 us)
Async XLA Ops:
  7.2 0.9 copy-start
  7.2 2.2 %copy-start.4 = (bf16[128,512]{1,0:T(8,128)(2,1)S(1)}, bf16[128,512]{1,0:T(8,128)(2,1)}, u32[]{:S(2)}) copy-start(bf16[128,512]{1,0:T(8,128)(2,1)} %param.10) | copy-start | bytes 393220
  7.2 38.7 %all-reduce.5.cloned.1.call-start = ((), (), s32[]{:S(2)}) async-start(), calls=%async_computation | async-start | bytes 524288 | tf_op jit(solution)/shard_map/psum | solution.py:43
  10.2 0.9 copy-start.2
  10.3 61.4 %all-gather.3.cloned.1.call-start = ((), (), s32[]{:S(2)}) async-start(), calls=%async_computation.1 | async-start | bytes 1310720 | tf_op jit(solution)/shard_map/all_gather | solution.py:100
  11.1 0.8 copy-start.5
  45.9 1.1 copy-start.1
  47.2 0.7 copy-start.6
  54.7 94.8 %all-reduce.7.cloned.1.call-start = ((), (), s32[]{:S(2)}) async-start(), calls=%async_computation.2 | async-start | bytes 1310720 | tf_op jit(solution)/shard_map/psum | solution.py:112
  149.5 2.0 %copy-start.3 = (f32[128,512]{1,0:T(8,128)S(1)}, f32[128,512]{1,0:T(8,128)}, u32[]{:S(2)}) copy-start(f32[128,512]{1,0:T(8,128)} %get-tuple-element.77) | copy-start | bytes 786436
Sparse Core Ops, SparseCore 0:
  10.9 34.9 all-reduce.4
  54.9 16.7 all-gather.2
  75.7 73.7 all-reduce.6
